TPU v7x, 32 devices: a whole 2x2x4 slice. The times are simulated.
32 devices in a mesh: mem: 4 (over x, core), lat: 8 (over z, y).
Axes of the slice: x: 2, y: 2, z: 4, core: 2. Of those that a mesh axis runs over, the one named last changes fastest.
Arguments:
- control: float32 [128, 16, 1024], P('mem', 'lat'), may hold values from -6 to 6
- ensemble: float32 [128, 4, 16, 1024], P('mem', None, 'lat'), may hold values from -0.72 to 0.72
- widths: int32 [16], P('lat'), may hold values from 0 to 4
- interp_source: int32 [4, 32, 2048], P(None, 'lat'), may hold values from 0 to 4095, as said below
- interp_weight: float32 [4, 32, 2048], P(None, 'lat'), may hold values from 0.1 to 0.5
- obs_mask: int32 [4, 32, 2048], P(None, 'lat'), may hold values 0 or 1
- innovation: float32 [4, 32, 2048], P(None, 'lat'), may hold values from -12 to 12
Outputs:
- control_next: float32 [128, 16, 1024], P('mem', 'lat')
Inputs may be any that keep to these rules, and one draw needn't show every extreme that they name: `interp_source`: for a fine point (j, i) in band b = j // 4 each value is (row - b * 2 + 1) * 1024 + column of a coarse cell inside the grid whose row differs from j // 2 by at most 1 and whose column differs from i // 2 by at most 2, cyclically modulo 1024.
All inputs are finite; a program needn't handle non-finite values. No bound on the sum of `obs_mask` on one device may be relied on, other than what follows from the above.
Results may differ from a plain program's by a relative error of at most 0.0001.
Values sent between devices are 32-bit elements; how exact they have to be, the bound alone decides.
A program may use at most 128 MiB of HBM per device.

v0:
```python
import jax
import jax.numpy as jnp
from jax import lax
from jax.sharding import PartitionSpec as P

WIDEST = 4
GRAD_STEPS = 2


C_MID = 0.5
C_SIDE = 0.25
STEP_SIZE = 0.5
HIGHEST_PRECISION = lax.Precision.HIGHEST


def padded_2(cells, sides, width):
    for axis, dim in sides:
        count = lax.axis_size(axis)
        ends = count - 1
        head = lax.slice_in_dim(cells, 0, width, axis=dim)
        tail = lax.slice_in_dim(cells, cells.shape[dim] - width, cells.shape[dim], axis=dim)
        cells = jnp.concatenate(
            [
                lax.ppermute(tail, axis, [(i, (i + 1) % count) for i in range(ends)]),
                cells,
                lax.ppermute(head, axis, [((i + 1) % count, i) for i in range(ends)]),
            ],
            axis=dim,
        )
    return cells


def lon_filter(source_field, widths):
    scaled = 1.0 / (2.0 * widths.astype(jnp.float32) + 1.0)
    summed = jnp.zeros_like(source_field)
    for offset in range(-WIDEST, WIDEST + 1):
        weight_row = jnp.where(abs(offset) <= widths, scaled, 0.0 * scaled)
        summed = summed + jnp.roll(source_field, offset, axis=-1) * weight_row[:, None]
    return summed


def lat_filter(source_field):
    padded = padded_2(source_field, (("lat", 1),), 1)
    return C_MID * source_field + C_SIDE * (padded[:, :-2] + padded[:, 2:])


def obs_stencil(fine_field):
    return (
        0.25 * jnp.roll(fine_field, 1, axis=-1)
        + 0.5 * fine_field
        + 0.25 * jnp.roll(fine_field, -1, axis=-1)
    )


def refine_field(coarse_part):
    slots, rows, cols = coarse_part.shape
    spread = jnp.broadcast_to(coarse_part[:, :, None, :, None], (slots, rows, 2, cols, 2))
    return spread.reshape(slots, 2 * rows, 2 * cols)


def coarsen_field(fine_portion):
    slots, rows, cols = fine_portion.shape
    return fine_portion.reshape(slots, rows // 2, 2, cols // 2, 2).sum(axis=(2, 4))


def offset_planes(interp_source, interp_weight, lon_count):
    fine_rows = interp_source.shape[1]
    fine_cols = interp_source.shape[2]
    input_row_index = interp_source // lon_count
    source_col = interp_source % lon_count
    parent_row = (jnp.arange(fine_rows, dtype=jnp.int32) // 2 + 1)[None, :, None]
    parent_col = (jnp.arange(fine_cols, dtype=jnp.int32) // 2)[None, None, :]
    row_shift = input_row_index - parent_row
    col_shift = (source_col - parent_col + 2) % lon_count - 2
    code = (row_shift + 1) * 5 + (col_shift + 2)
    planes = []
    for number in range(15):
        planes.append(jnp.sum(jnp.where(code == number, interp_weight, 0.0), axis=0))
    return planes


def local(control, ensemble, widths, interp_source, interp_weight, obs_mask, innovation):
    slot_count = ensemble.shape[1]
    count_of_rows = control.shape[1]
    lon_count = control.shape[2]
    obs_weight = obs_mask.astype(jnp.float32)
    slot_share = slot_count // lax.axis_size("mem")
    first_slot = lax.axis_index("mem") * slot_share
    obs_weight = lax.dynamic_slice_in_dim(obs_weight, first_slot, slot_share, 0)
    target = lax.dynamic_slice_in_dim(innovation, first_slot, slot_share, 0)
    planes = offset_planes(interp_source, interp_weight, lon_count)
    control_now = control
    for iteration in range(GRAD_STEPS):
        forward = lat_filter(lon_filter(control_now, widths))
        partial_sum = jnp.einsum("mtri,mri->tri", ensemble, forward, precision=HIGHEST_PRECISION)
        coarse = lax.psum_scatter(partial_sum, "mem", scatter_dimension=0, tiled=True)
        window = padded_2(coarse, (("lat", 1),), 1)
        fine_field = jnp.zeros((slot_share, 2 * count_of_rows, 2 * lon_count), jnp.float32)
        for row_shift in range(-1, 2):
            band_rows = window[:, 1 + row_shift : 1 + row_shift + count_of_rows]
            for col_shift in range(-2, 3):
                shifted = jnp.roll(band_rows, -col_shift, axis=-1)
                fine_field = fine_field + planes[(row_shift + 1) * 5 + col_shift + 2][
                    None
                ] * refine_field(shifted)
        misfit = obs_weight * (obs_stencil(fine_field) - target)
        fine_grid_return = obs_stencil(misfit)
        landed = jnp.zeros((slot_share, count_of_rows + 2, lon_count), jnp.float32)
        for row_shift in range(-1, 2):
            for col_shift in range(-2, 3):
                collected_return = coarsen_field(
                    planes[(row_shift + 1) * 5 + col_shift + 2][None] * fine_grid_return
                )
                rolled = jnp.roll(collected_return, col_shift, axis=-1)
                landed = landed + jnp.pad(rolled, ((0, 0), (1 + row_shift, 1 - row_shift), (0, 0)))
        rim_rows = jnp.concatenate([landed[:, :1], landed[:, -1:]], axis=1)
        arrived = padded_2(rim_rows, (("lat", 1),), 1)
        coarse_back = landed[:, 1:-1]
        coarse_back = coarse_back.at[:, 0].add(arrived[:, 0]).at[:, -1].add(arrived[:, 3])
        coarse_back = lax.all_gather(coarse_back, "mem", axis=0, tiled=True)
        member_back = jnp.einsum(
            "mtri,tri->mri", ensemble, coarse_back, precision=HIGHEST_PRECISION
        )
        gradient = control_now + lon_filter(lat_filter(member_back), widths)
        control_now = control_now - STEP_SIZE * gradient
    return control_now


def solution(mesh):
    in_specs = (
        P("mem", "lat", None),
        P("mem", None, "lat", None),
        P("lat"),
        P(None, "lat", None),
        P(None, "lat", None),
        P(None, "lat", None),
        P(None, "lat", None),
    )
    out_specs = P("mem", "lat", None)
    return jax.shard_map(local, mesh=mesh, in_specs=in_specs, out_specs=out_specs, check_vma=False)
```

profile of v0, /device:TPU:0, one launch (start us, length us, event | category | flops | bytes accessed | tf_op | source)
XLA Modules:
  0.0 411.8 jit_solution(15525623656420890092)
XLA Ops:
  8.8 4.9 %collective-permute-start = (f32[32,1,1024]{2,1,0:T(1,128)S(1)}, f32[32,1,1024]{2,1,0:T(1,128)S(1)}, u32[]{:S(2)}, u32[]{:S(2)}) collective-permute-start(f32[32,1,1024]{2,1,0:T(1,128)S(1)} %get-tuple-element.128), channel_id=1, source_target_pairs={{0,1},{1,2},{2,3},{3,4},{4,5},{5,6},{6,7},{8,9},{9,10},{10,11},{11... | collective-permute-start | bytes 393224 | tf_op jit(solution)/shard_map/ppermute | solution.py:24
  17.3 3.3 collective-permute-done.1
  21.6 10.3 %all-reduce.30 = f32[4,2,1024]{2,1,0:T(2,128)S(1)} all-reduce(f32[4,2,1024]{2,1,0:T(2,128)S(1)} %bitcast.376), channel_id=2, replica_groups=mesh['mem'=4,'lat'=8] {'mem'}, use_global_device_ids=true, to_apply=%region_1.2.clone | all-reduce | flops 8192 | bytes 65536
  35.6 4.3 %collective-permute-start.2 = (f32[1,1,1024]{2,1,0:T(1,128)}, f32[1,1,1024]{2,1,0:T(1,128)S(1)}, u32[]{:S(2)}, u32[]{:S(2)}) collective-permute-start(f32[1,1,1024]{2,1,0:T(1,128)} %get-tuple-element.200), channel_id=1, source_target_pairs={{0,1},{1,2},{2,3},{3,4},{4,5},{5,6},{6,7},{8,9},{9,10},{10,11},{11... | collective-permute-start | bytes 12296 | tf_op jit(solution)/shard_map/ppermute | solution.py:24
  156.5 4.5 %collective-permute-start.4 = (f32[1,1,1024]{2,1,0:T(1,128)S(1)}, f32[1,1,1024]{2,1,0:T(1,128)S(1)}, u32[]{:S(2)}, u32[]{:S(2)}) collective-permute-start(f32[1,1,1024]{2,1,0:T(1,128)S(1)} %get-tuple-element.213), channel_id=1, source_target_pairs={{0,1},{1,2},{2,3},{3,4},{4,5},{5,6},{6,7},{8,9},{9,10},{10,11},{11... | collective-permute-start | bytes 12296 | tf_op jit(solution)/shard_map/ppermute | solution.py:24
  162.4 4.4 %collective-permute-done.5 = f32[1,1,1024]{2,1,0:T(1,128)S(1)} collective-permute-done((f32[1,1,1024]{2,1,0:T(1,128)S(1)}, f32[1,1,1024]{2,1,0:T(1,128)S(1)}, u32[]{:S(2)}, u32[]{:S(2)}) %collective-permute-start.5) | collective-permute-done | bytes 4128 | tf_op jit(solution)/shard_map/ppermute | solution.py:26
  166.9 5.4 %all_gather.6 = f32[4,2,1024]{2,1,0:T(2,128)S(1)} all-gather(f32[1,2,1024]{2,1,0:T(2,128)S(1)} %scatter-add.15), channel_id=1, replica_groups=mesh['mem'=4,'lat'=8] {'mem'}, dimensions={0}, use_global_device_ids=true | all-gather | bytes 40960 | tf_op jit(solution)/shard_map/all_gather | solution.py:120
  173.1 4.8 %collective-permute-start.6 = (f32[32,1,1024]{2,1,0:T(1,128)S(1)}, f32[32,1,1024]{2,1,0:T(1,128)S(1)}, u32[]{:S(2)}, u32[]{:S(2)}) collective-permute-start(f32[32,1,1024]{2,1,0:T(1,128)S(1)} %get-tuple-element.126), channel_id=1, source_target_pairs={{0,1},{1,2},{2,3},{3,4},{4,5},{5,6},{6,7},{8,9},{9,10},{10,11},{11... | collective-permute-start | bytes 393224 | tf_op jit(solution)/shard_map/ppermute | solution.py:24
  181.1 4.1 %collective-permute-done.7 = f32[32,1,1024]{2,1,0:T(1,128)S(1)} collective-permute-done((f32[32,1,1024]{2,1,0:T(1,128)S(1)}, f32[32,1,1024]{2,1,0:T(1,128)S(1)}, u32[]{:S(2)}, u32[]{:S(2)}) %collective-permute-start.7) | collective-permute-done | bytes 131104 | tf_op jit(solution)/shard_map/ppermute | solution.py:26
  199.2 4.4 %collective-permute-done.9 = f32[32,1,1024]{2,1,0:T(1,128)S(1)} collective-permute-done((f32[32,1,1024]{2,1,0:T(1,128)S(1)}, f32[32,1,1024]{2,1,0:T(1,128)S(1)}, u32[]{:S(2)}, u32[]{:S(2)}) %collective-permute-start.9) | collective-permute-done | bytes 131104 | tf_op jit(solution)/shard_map/ppermute | solution.py:26
  204.6 10.3 %all-reduce.31 = f32[4,2,1024]{2,1,0:T(2,128)S(1)} all-reduce(f32[4,2,1024]{2,1,0:T(2,128)S(1)} %bitcast.377), channel_id=3, replica_groups=mesh['mem'=4,'lat'=8] {'mem'}, use_global_device_ids=true, to_apply=%region_31.32.clone | all-reduce | flops 8192 | bytes 65536
  219.2 4.5 %collective-permute-start.10 = (f32[1,1,1024]{2,1,0:T(1,128)S(1)}, f32[1,1,1024]{2,1,0:T(1,128)S(1)}, u32[]{:S(2)}, u32[]{:S(2)}) collective-permute-start(f32[1,1,1024]{2,1,0:T(1,128)S(1)} %get-tuple-element.168), channel_id=1, source_target_pairs={{0,1},{1,2},{2,3},{3,4},{4,5},{5,6},{6,7},{8,9},{9,10},{10,11},{11... | collective-permute-start | bytes 12296 | tf_op jit(solution)/shard_map/ppermute | solution.py:24
  295.6 3.7 reshape.1670
  301.3 3.5 reshape.1669
  306.7 3.5 reshape.1665
  312.2 3.5 reshape.1664
  317.7 3.5 reshape.1660
  323.2 3.5 reshape.1659
  328.7 3.5 reshape.1666
  334.1 3.5 reshape.1661
  339.5 3.8 reshape.1672
  345.3 3.5 reshape.1671
  350.7 3.5 reshape.1668
  356.2 3.5 reshape.1667
  361.7 3.5 reshape.1663
  367.1 3.5 reshape.1662
  372.6 3.5 reshape.1673
  378.2 4.5 %collective-permute-start.12 = (f32[1,1,1024]{2,1,0:T(1,128)S(1)}, f32[1,1,1024]{2,1,0:T(1,128)S(1)}, u32[]{:S(2)}, u32[]{:S(2)}) collective-permute-start(f32[1,1,1024]{2,1,0:T(1,128)S(1)} %get-tuple-element.211), channel_id=1, source_target_pairs={{0,1},{1,2},{2,3},{3,4},{4,5},{5,6},{6,7},{8,9},{9,10},{10,11},{11... | collective-permute-start | bytes 12296 | tf_op jit(solution)/shard_map/ppermute | solution.py:24
  384.2 4.1 collective-permute-done.13
  388.4 5.2 %all_gather.7 = f32[4,2,1024]{2,1,0:T(2,128)S(1)} all-gather(f32[1,2,1024]{2,1,0:T(2,128)S(1)} %scatter-add.19), channel_id=1, replica_groups=mesh['mem'=4,'lat'=8] {'mem'}, dimensions={0}, use_global_device_ids=true | all-gather | bytes 40960 | tf_op jit(solution)/shard_map/all_gather | solution.py:120
  394.3 4.7 %collective-permute-start.14 = (f32[32,1,1024]{2,1,0:T(1,128)S(1)}, f32[32,1,1024]{2,1,0:T(1,128)S(1)}, u32[]{:S(2)}, u32[]{:S(2)}) collective-permute-start(f32[32,1,1024]{2,1,0:T(1,128)S(1)} %get-tuple-element.90), channel_id=1, source_target_pairs={{0,1},{1,2},{2,3},{3,4},{4,5},{5,6},{6,7},{8,9},{9,10},{10,11},{11... | collective-permute-start | bytes 393224 | tf_op jit(solution)/shard_map/ppermute | solution.py:24
  402.2 4.1 %collective-permute-done.15 = f32[32,1,1024]{2,1,0:T(1,128)S(1)} collective-permute-done((f32[32,1,1024]{2,1,0:T(1,128)S(1)}, f32[32,1,1024]{2,1,0:T(1,128)S(1)}, u32[]{:S(2)}, u32[]{:S(2)}) %collective-permute-start.15) | collective-permute-done | bytes 131104 | tf_op jit(solution)/shard_map/ppermute | solution.py:26
  (346 shorter events, 269.9 us)
Async XLA Ops:
  0.0 6.3 %copy-start = (f32[32,2,1024]{2,1,0:T(2,128)S(1)}, f32[32,2,1024]{2,1,0:T(2,128)}, u32[]{:S(2)}) copy-start(f32[32,2,1024]{2,1,0:T(2,128)} %param.15) | copy-start | bytes 786436
  6.7 8.4 %copy-start.13 = (f32[4,4,2048]{2,1,0:T(4,128)S(1)}, f32[4,4,2048]{2,1,0:T(4,128)}, u32[]{:S(2)}) copy-start(f32[4,4,2048]{2,1,0:T(4,128)} %param.19) | copy-start | bytes 393220
  6.7 8.4 %copy-start.14 = (s32[4,4,2048]{2,1,0:T(4,128)S(1)}, s32[4,4,2048]{2,1,0:T(4,128)}, u32[]{:S(2)}) copy-start(s32[4,4,2048]{2,1,0:T(4,128)} %param.18) | copy-start | bytes 393220
  7.1 9.6 %copy-start.30 = (f32[2]{0:T(128)}, f32[2]{0:T(128)S(1)}, u32[]{:S(2)}) copy-start(f32[2]{0:T(128)S(1)} %get-tuple-element.72) | copy-start | bytes 28
  7.1 9.6 %copy-start.22 = (f32[2]{0:T(128)}, f32[2]{0:T(128)S(1)}, u32[]{:S(2)}) copy-start(f32[2]{0:T(128)S(1)} %get-tuple-element.268) | copy-start | bytes 28
  7.1 9.6 %copy-start.24 = (f32[2]{0:T(128)}, f32[2]{0:T(128)S(1)}, u32[]{:S(2)}) copy-start(f32[2]{0:T(128)S(1)} %get-tuple-element.269) | copy-start | bytes 28
  7.1 9.6 %copy-start.26 = (f32[2]{0:T(128)}, f32[2]{0:T(128)S(1)}, u32[]{:S(2)}) copy-start(f32[2]{0:T(128)S(1)} %get-tuple-element.270) | copy-start | bytes 28
  7.1 9.6 %copy-start.28 = (f32[2]{0:T(128)}, f32[2]{0:T(128)S(1)}, u32[]{:S(2)}) copy-start(f32[2]{0:T(128)S(1)} %get-tuple-element.271) | copy-start | bytes 28
  7.1 9.6 %copy-start.33 = (u32[32]{0:T(128)S(1)}, u32[32]{0:T(128)}, u32[]{:S(2)}) copy-start(u32[32]{0:T(128)} %constant.279) | copy-start | bytes 388
  7.1 14.0 %copy-start.1 = (f32[32,4,2,1024]{3,2,1,0:T(2,128)S(1)}, f32[32,4,2,1024]{3,2,1,0:T(2,128)}, u32[]{:S(2)}) copy-start(f32[32,4,2,1024]{3,2,1,0:T(2,128)} %param.16) | copy-start | bytes 3145732
  8.8 8.5 %collective-permute-start = (f32[32,1,1024]{2,1,0:T(1,128)S(1)}, f32[32,1,1024]{2,1,0:T(1,128)S(1)}, u32[]{:S(2)}, u32[]{:S(2)}) collective-permute-start(f32[32,1,1024]{2,1,0:T(1,128)S(1)} %get-tuple-element.128), channel_id=1, source_target_pairs={{0,1},{1,2},{2,3},{3,4},{4,5},{5,6},{6,7},{8,9},{9,10},{10,11},{11... | collective-permute-start | bytes 393224 | tf_op jit(solution)/shard_map/ppermute | solution.py:24
  13.7 6.9 %collective-permute-start.1 = (f32[32,1,1024]{2,1,0:T(1,128)S(1)}, f32[32,1,1024]{2,1,0:T(1,128)S(1)}, u32[]{:S(2)}, u32[]{:S(2)}) collective-permute-start(f32[32,1,1024]{2,1,0:T(1,128)S(1)} %get-tuple-element.129), channel_id=1, source_target_pairs={{1,0},{2,1},{3,2},{4,3},{5,4},{6,5},{7,6},{9,8},{10,9},{11,10},{12... | collective-permute-start | bytes 393224 | tf_op jit(solution)/shard_map/ppermute | solution.py:26
  35.6 22.6 %collective-permute-start.2 = (f32[1,1,1024]{2,1,0:T(1,128)}, f32[1,1,1024]{2,1,0:T(1,128)S(1)}, u32[]{:S(2)}, u32[]{:S(2)}) collective-permute-start(f32[1,1,1024]{2,1,0:T(1,128)} %get-tuple-element.200), channel_id=1, source_target_pairs={{0,1},{1,2},{2,3},{3,4},{4,5},{5,6},{6,7},{8,9},{9,10},{10,11},{11... | collective-permute-start | bytes 12296 | tf_op jit(solution)/shard_map/ppermute | solution.py:24
  39.9 18.3 %collective-permute-start.3 = (f32[1,1,1024]{2,1,0:T(1,128)}, f32[1,1,1024]{2,1,0:T(1,128)S(1)}, u32[]{:S(2)}, u32[]{:S(2)}) collective-permute-start(f32[1,1,1024]{2,1,0:T(1,128)} %get-tuple-element.201), channel_id=1, source_target_pairs={{1,0},{2,1},{3,2},{4,3},{5,4},{6,5},{7,6},{9,8},{10,9},{11,10},{12... | collective-permute-start | bytes 12296 | tf_op jit(solution)/shard_map/ppermute | solution.py:26
  156.5 5.9 %collective-permute-start.4 = (f32[1,1,1024]{2,1,0:T(1,128)S(1)}, f32[1,1,1024]{2,1,0:T(1,128)S(1)}, u32[]{:S(2)}, u32[]{:S(2)}) collective-permute-start(f32[1,1,1024]{2,1,0:T(1,128)S(1)} %get-tuple-element.213), channel_id=1, source_target_pairs={{0,1},{1,2},{2,3},{3,4},{4,5},{5,6},{6,7},{8,9},{9,10},{10,11},{11... | collective-permute-start | bytes 12296 | tf_op jit(solution)/shard_map/ppermute | solution.py:24
  161.0 5.8 %collective-permute-start.5 = (f32[1,1,1024]{2,1,0:T(1,128)S(1)}, f32[1,1,1024]{2,1,0:T(1,128)S(1)}, u32[]{:S(2)}, u32[]{:S(2)}) collective-permute-start(f32[1,1,1024]{2,1,0:T(1,128)S(1)} %get-tuple-element.212), channel_id=1, source_target_pairs={{1,0},{2,1},{3,2},{4,3},{5,4},{6,5},{7,6},{9,8},{10,9},{11,10},{12... | collective-permute-start | bytes 12296 | tf_op jit(solution)/shard_map/ppermute | solution.py:26
  173.1 8.1 %collective-permute-start.6 = (f32[32,1,1024]{2,1,0:T(1,128)S(1)}, f32[32,1,1024]{2,1,0:T(1,128)S(1)}, u32[]{:S(2)}, u32[]{:S(2)}) collective-permute-start(f32[32,1,1024]{2,1,0:T(1,128)S(1)} %get-tuple-element.126), channel_id=1, source_target_pairs={{0,1},{1,2},{2,3},{3,4},{4,5},{5,6},{6,7},{8,9},{9,10},{10,11},{11... | collective-permute-start | bytes 393224 | tf_op jit(solution)/shard_map/ppermute | solution.py:24
  177.9 7.4 %collective-permute-start.7 = (f32[32,1,1024]{2,1,0:T(1,128)S(1)}, f32[32,1,1024]{2,1,0:T(1,128)S(1)}, u32[]{:S(2)}, u32[]{:S(2)}) collective-permute-start(f32[32,1,1024]{2,1,0:T(1,128)S(1)} %get-tuple-element.127), channel_id=1, source_target_pairs={{1,0},{2,1},{3,2},{4,3},{5,4},{6,5},{7,6},{9,8},{10,9},{11,10},{12... | collective-permute-start | bytes 393224 | tf_op jit(solution)/shard_map/ppermute | solution.py:26
  193.5 5.7 %collective-permute-start.8 = (f32[32,1,1024]{2,1,0:T(1,128)S(1)}, f32[32,1,1024]{2,1,0:T(1,128)S(1)}, u32[]{:S(2)}, u32[]{:S(2)}) collective-permute-start(f32[32,1,1024]{2,1,0:T(1,128)S(1)} %get-tuple-element.92), channel_id=1, source_target_pairs={{0,1},{1,2},{2,3},{3,4},{4,5},{5,6},{6,7},{8,9},{9,10},{10,11},{11... | collective-permute-start | bytes 393224 | tf_op jit(solution)/shard_map/ppermute | solution.py:24
  196.7 6.9 %collective-permute-start.9 = (f32[32,1,1024]{2,1,0:T(1,128)S(1)}, f32[32,1,1024]{2,1,0:T(1,128)S(1)}, u32[]{:S(2)}, u32[]{:S(2)}) collective-permute-start(f32[32,1,1024]{2,1,0:T(1,128)S(1)} %get-tuple-element.93), channel_id=1, source_target_pairs={{1,0},{2,1},{3,2},{4,3},{5,4},{6,5},{7,6},{9,8},{10,9},{11,10},{12... | collective-permute-start | bytes 393224 | tf_op jit(solution)/shard_map/ppermute | solution.py:26
  219.2 28.9 %collective-permute-start.10 = (f32[1,1,1024]{2,1,0:T(1,128)S(1)}, f32[1,1,1024]{2,1,0:T(1,128)S(1)}, u32[]{:S(2)}, u32[]{:S(2)}) collective-permute-start(f32[1,1,1024]{2,1,0:T(1,128)S(1)} %get-tuple-element.168), channel_id=1, source_target_pairs={{0,1},{1,2},{2,3},{3,4},{4,5},{5,6},{6,7},{8,9},{9,10},{10,11},{11... | collective-permute-start | bytes 12296 | tf_op jit(solution)/shard_map/ppermute | solution.py:24
  223.7 24.4 %collective-permute-start.11 = (f32[1,1,1024]{2,1,0:T(1,128)S(1)}, f32[1,1,1024]{2,1,0:T(1,128)S(1)}, u32[]{:S(2)}, u32[]{:S(2)}) collective-permute-start(f32[1,1,1024]{2,1,0:T(1,128)S(1)} %get-tuple-element.169), channel_id=1, source_target_pairs={{1,0},{2,1},{3,2},{4,3},{5,4},{6,5},{7,6},{9,8},{10,9},{11,10},{12... | collective-permute-start | bytes 12296 | tf_op jit(solution)/shard_map/ppermute | solution.py:26
  289.4 4.6 %copy-start.2 = (f32[4,2048]{1,0:T(4,128)S(1)}, f32[4,2048]{1,0:T(4,128)}, u32[]{:S(2)}) copy-start(f32[4,2048]{1,0:T(4,128)} %get-tuple-element.56) | copy-start | bytes 98308
  289.4 4.6 %copy-start.3 = (f32[4,2048]{1,0:T(4,128)S(1)}, f32[4,2048]{1,0:T(4,128)}, u32[]{:S(2)}) copy-start(f32[4,2048]{1,0:T(4,128)} %get-tuple-element.57) | copy-start | bytes 98308
  289.4 4.6 %copy-start.4 = (f32[4,2048]{1,0:T(4,128)S(1)}, f32[4,2048]{1,0:T(4,128)}, u32[]{:S(2)}) copy-start(f32[4,2048]{1,0:T(4,128)} %get-tuple-element.58) | copy-start | bytes 98308
  289.4 4.6 %copy-start.5 = (f32[4,2048]{1,0:T(4,128)S(1)}, f32[4,2048]{1,0:T(4,128)}, u32[]{:S(2)}) copy-start(f32[4,2048]{1,0:T(4,128)} %get-tuple-element.59) | copy-start | bytes 98308
  289.4 4.6 %copy-start.6 = (f32[4,2048]{1,0:T(4,128)S(1)}, f32[4,2048]{1,0:T(4,128)}, u32[]{:S(2)}) copy-start(f32[4,2048]{1,0:T(4,128)} %get-tuple-element.60) | copy-start | bytes 98308
  289.4 4.6 %copy-start.7 = (f32[4,2048]{1,0:T(4,128)S(1)}, f32[4,2048]{1,0:T(4,128)}, u32[]{:S(2)}) copy-start(f32[4,2048]{1,0:T(4,128)} %get-tuple-element.61) | copy-start | bytes 98308
  378.2 5.9 %collective-permute-start.12 = (f32[1,1,1024]{2,1,0:T(1,128)S(1)}, f32[1,1,1024]{2,1,0:T(1,128)S(1)}, u32[]{:S(2)}, u32[]{:S(2)}) collective-permute-start(f32[1,1,1024]{2,1,0:T(1,128)S(1)} %get-tuple-element.211), channel_id=1, source_target_pairs={{0,1},{1,2},{2,3},{3,4},{4,5},{5,6},{6,7},{8,9},{9,10},{10,11},{11... | collective-permute-start | bytes 12296 | tf_op jit(solution)/shard_map/ppermute | solution.py:24
  382.8 5.5 %collective-permute-start.13 = (f32[1,1,1024]{2,1,0:T(1,128)S(1)}, f32[1,1,1024]{2,1,0:T(1,128)S(1)}, u32[]{:S(2)}, u32[]{:S(2)}) collective-permute-start(f32[1,1,1024]{2,1,0:T(1,128)S(1)} %get-tuple-element.210), channel_id=1, source_target_pairs={{1,0},{2,1},{3,2},{4,3},{5,4},{6,5},{7,6},{9,8},{10,9},{11,10},{12... | collective-permute-start | bytes 12296 | tf_op jit(solution)/shard_map/ppermute | solution.py:26
  394.3 7.9 %collective-permute-start.14 = (f32[32,1,1024]{2,1,0:T(1,128)S(1)}, f32[32,1,1024]{2,1,0:T(1,128)S(1)}, u32[]{:S(2)}, u32[]{:S(2)}) collective-permute-start(f32[32,1,1024]{2,1,0:T(1,128)S(1)} %get-tuple-element.90), channel_id=1, source_target_pairs={{0,1},{1,2},{2,3},{3,4},{4,5},{5,6},{6,7},{8,9},{9,10},{10,11},{11... | collective-permute-start | bytes 393224 | tf_op jit(solution)/shard_map/ppermute | solution.py:24
  399.0 7.4 %collective-permute-start.15 = (f32[32,1,1024]{2,1,0:T(1,128)S(1)}, f32[32,1,1024]{2,1,0:T(1,128)S(1)}, u32[]{:S(2)}, u32[]{:S(2)}) collective-permute-start(f32[32,1,1024]{2,1,0:T(1,128)S(1)} %get-tuple-element.91), channel_id=1, source_target_pairs={{1,0},{2,1},{3,2},{4,3},{5,4},{6,5},{7,6},{9,8},{10,9},{11,10},{12... | collective-permute-start | bytes 393224 | tf_op jit(solution)/shard_map/ppermute | solution.py:26
  (18 other events, 49.0 us)
where the time goes:
time: 420 us; the launch traced here: 412 us
  local copies, waits for them, and re-layouts  237 us (56%)
  other arithmetic  66.2 us (16%)
  starting transfers between devices  46.6 us (11%)
  blocking collectives  31.1 us (7%)
  waiting for transfers between devices  29.3 us (7%)
    broadcast_in_dim x62, local copies, waits for them, and re-layouts, refine_field(): jnp.broadcast_to(coarse_part[:, :, None, :, None], (slots, rows, 2, cols,...  105 us
    reshape x30, local copies, waits for them, and re-layouts, coarsen_field(): fine_portion.reshape(slots, rows // 2, 2, cols // 2, 2).sum(axis=(2, 4))  95.4 us
    reduce_sum x30, other arithmetic, coarsen_field(): fine_portion.reshape(slots, rows // 2, 2, cols // 2, 2).sum(axis=(2, 4))  38.8 us
    ppermute x8, starting transfers between devices, padded_2(): lax.ppermute(tail, axis, [(i, (i + 1) % count) for i in range(ends)])  35.5 us
    ppermute x8, waiting for transfers between devices, padded_2(): lax.ppermute(head, axis, [((i + 1) % count, i) for i in range(ends)])  24.4 us
    unnamed x2, blocking collectives  20.5 us
    slice x36, local copies, waits for them, and re-layouts, local(): rolled = jnp.roll(collected_return, col_shift, axis=-1)  14.3 us
    slice x32, local copies, waits for them, and re-layouts, lon_filter(): jnp.roll(source_field, offset, axis=-1) * weight_row[:, None]  12.2 us
  transfers between devices with their start and end apart: 16, of which 9 were waited for; matrix products, arithmetic and copies ran while one was open for 10% of the time, Pallas kernels for 0%

commit v1 on v0

v1 whole, which is shorter than its diff:
```python
import functools

import jax
import jax.numpy as jnp
from jax import lax
from jax.experimental import pallas as pl
from jax.experimental.pallas import tpu as pltpu
from jax.sharding import PartitionSpec as P

WIDEST = 4
GRAD_STEPS = 2
C_MID = 0.5
C_SIDE = 0.25
STEP_SIZE = 0.5
GROUP = 8
LANES = 128
REACH = 2
COLS = 2 * REACH + 1
MESH = pl.DeviceIdType.MESH


def rolled(x, shift):
    shift = shift % x.shape[-1]
    return x if shift == 0 else pltpu.roll(x, shift, x.ndim - 1)


def lon_filter(x, weights):
    total = x * weights[0]
    for k in range(1, WIDEST + 1):
        total = total + (rolled(x, k) + rolled(x, -k)) * weights[k]
    return total


def stencil(even, odd):
    return (
        0.25 * (rolled(odd, 1) + odd) + 0.5 * even,
        0.25 * (even + rolled(even, -1)) + 0.5 * odd,
    )


def kernel(
    sizes,
    widths,
    control,
    ensemble,
    source,
    weight,
    obs_mask,
    innovation,
    out,
    ens,
    now,
    edge,
    halo,
    forward,
    result,
    rows_in,
    rows_out,
    planes,
    mask,
    target,
    fine,
    part,
    peers,
    coarse,
    rim,
    land,
    land_rim,
    back,
    load_sem,
    edge_send,
    edge_recv,
    peer_send,
    peer_recv,
    rim_send,
    rim_recv,
    land_send,
    land_recv,
):
    slots, members, rows, lon, mem_count, lat_count = sizes
    groups = members // GROUP
    me_mem = lax.axis_index("mem")
    me_lat = lax.axis_index("lat")
    has = (me_lat > 0, me_lat < lat_count - 1)
    beside = (me_lat - 1, me_lat + 1)

    loads = []
    for r in range(rows):
        loads.append(pltpu.make_async_copy(control.at[:, r, :], now.at[r], load_sem.at[r]))
        loads[-1].start()
    for t in range(slots):
        for r in range(rows):
            number = rows + t * rows + r
            loads.append(
                pltpu.make_async_copy(ensemble.at[:, t, r, :], ens.at[t, r], load_sem.at[number])
            )
            loads[-1].start()

    barrier = pltpu.get_barrier_semaphore()
    for d in range(1, mem_count):
        pl.semaphore_signal(
            barrier,
            inc=1,
            device_id={"mem": lax.rem(me_mem + d, mem_count)},
            device_id_type=MESH,
        )
    for side in range(2):

        @pl.when(has[side])
        def _():
            pl.semaphore_signal(
                barrier, inc=1, device_id={"lat": beside[side]}, device_id_type=MESH
            )

    pl.semaphore_wait(
        barrier, mem_count - 1 + has[0].astype(jnp.int32) + has[1].astype(jnp.int32)
    )

    def to_side(side, src, dst, send, recv):
        return pltpu.make_async_remote_copy(
            src_ref=src,
            dst_ref=dst,
            send_sem=send,
            recv_sem=recv,
            device_id={"lat": beside[side]},
            device_id_type=MESH,
        )

    def edge_copy(phase, side, g):
        row = 0 if side == 0 else rows - 1
        part_of = pl.ds(g * GROUP, GROUP)
        return to_side(
            side,
            edge.at[phase, row, part_of],
            halo.at[phase, 1 - side, part_of],
            edge_send.at[phase, side, g],
            edge_recv.at[phase, 1 - side, g],
        )

    def edge_start(phase, g):
        for side in range(2):

            @pl.when(has[side])
            def _():
                edge_copy(phase, side, g).start()

    def edge_wait(phase, g):
        for side in range(2):

            @pl.when(has[side])
            def _():
                edge_copy(phase, 1 - side, g).wait_recv()

    def edge_done(phase):
        for g in range(groups):
            for side in range(2):

                @pl.when(has[side])
                def _():
                    edge_copy(phase, side, g).wait_send()

    weights = []
    for r in range(rows):
        width = widths[r]
        scale = jnp.float32(1.0 / (2 * WIDEST + 1))
        for w in range(WIDEST):
            scale = jnp.where(width == w, jnp.float32(1.0 / (2 * w + 1)), scale)
        weights.append(
            [jnp.where(width >= k, scale, jnp.float32(0.0)) for k in range(WIDEST + 1)]
        )

    def spread(phase, g):
        part_of = pl.ds(g * GROUP, GROUP)
        own = [edge[phase, r, part_of, :] for r in range(rows)]
        padded = [halo[phase, 0, part_of, :], *own, halo[phase, 1, part_of, :]]
        return [
            C_MID * padded[r + 1] + C_SIDE * (padded[r] + padded[r + 2]) for r in range(rows)
        ]

    for side in range(2):

        @pl.when(jnp.logical_not(has[side]))
        def _():
            for phase in range(2 * GRAD_STEPS):
                halo[phase, side] = jnp.zeros((members, lon), jnp.float32)
            for step in range(GRAD_STEPS):
                rim[step, side] = jnp.zeros((slots, lon), jnp.float32)
                land_rim[step, side] = jnp.zeros((slots, lon), jnp.float32)

    for r in range(rows):
        loads[r].wait()
    for g in range(groups):
        part_of = pl.ds(g * GROUP, GROUP)
        for r in range(rows):
            edge[0, r, part_of, :] = lon_filter(now[r, part_of, :], weights[r])
        edge_start(0, g)

    fine_rows = 2 * rows
    four = source.shape[0]
    for s in range(four):
        rows_in[pl.ds(s * fine_rows, fine_rows), :] = source[s].astype(jnp.float32)
        rows_in[pl.ds((four + s) * fine_rows, fine_rows), :] = weight[s]
    for r in range(rows):
        for jj in range(2):
            top = 2 * four * fine_rows + (r * 2 + jj) * slots
            rows_in[pl.ds(top, slots), :] = obs_mask[:, 2 * r + jj, :].astype(jnp.float32)
            top = top + rows * 2 * slots
            rows_in[pl.ds(top, slots), :] = innovation[:, 2 * r + jj, :]
    line = lax.broadcasted_iota(jnp.int32, (2 * LANES, 2 * LANES), 0)
    column = lax.broadcasted_iota(jnp.int32, (2 * LANES, 2 * LANES), 1)
    wanted = jnp.where(column < LANES, 2 * column, 2 * (column - LANES) + 1)
    pick = jnp.where(line == wanted, 1.0, 0.0).astype(jnp.float32)
    for block in range(lon // LANES):
        both = jnp.dot(
            rows_in[:, pl.ds(block * 2 * LANES, 2 * LANES)],
            pick,
            precision=lax.Precision.HIGHEST,
            preferred_element_type=jnp.float32,
        )
        rows_out[0, :, pl.ds(block * LANES, LANES)] = both[:, :LANES]
        rows_out[1, :, pl.ds(block * LANES, LANES)] = both[:, LANES:]
    across = lax.broadcasted_iota(jnp.int32, (2 * slots, lon), 1).astype(jnp.float32)
    for r in range(rows):
        for p in range(2):
            top = 2 * four * fine_rows + r * 2 * slots
            mask[r, p] = rows_out[p, pl.ds(top, 2 * slots), :]
            target[r, p] = rows_out[p, pl.ds(top + rows * 2 * slots, 2 * slots), :]
            codes, heavy = [], []
            for s in range(four):
                pair_code, pair_weight = [], []
                for jj in range(2):
                    at = s * fine_rows + 2 * r + jj
                    pair_code.append(
                        jnp.broadcast_to(rows_out[p, pl.ds(at, 1), :], (slots, lon))
                    )
                    at = at + four * fine_rows
                    pair_weight.append(
                        jnp.broadcast_to(rows_out[p, pl.ds(at, 1), :], (slots, lon))
                    )
                flat = jnp.floor(jnp.concatenate(pair_code, axis=0) + 0.5)
                line_of = jnp.floor((flat + 0.5) * (1.0 / lon))
                shift = flat - line_of * lon - across + REACH
                shift = jnp.where(shift < 0.0, shift + lon, shift)
                shift = jnp.where(shift >= lon, shift - lon, shift)
                codes.append((line_of - r) * COLS + shift)
                heavy.append(jnp.concatenate(pair_weight, axis=0))
            for number in range(3 * COLS):
                total = jnp.where(codes[0] == number, heavy[0], 0.0)
                for s in range(1, four):
                    total = total + jnp.where(codes[s] == number, heavy[s], 0.0)
                planes[number, r, p] = total

    for load in loads[rows:]:
        load.wait()

    for step in range(GRAD_STEPS):
        for g in range(groups):
            edge_wait(2 * step, g)
            spreads = spread(2 * step, g)
            for r in range(rows):
                forward[r, pl.ds(g * GROUP, GROUP), :] = spreads[r]
        for r in range(rows):
            for t in range(slots):
                total = jnp.zeros((GROUP, lon), jnp.float32)
                for g in range(groups):
                    part_of = pl.ds(g * GROUP, GROUP)
                    total = total + ens[t, r, part_of, :] * forward[r, part_of, :]
                part[step, r, pl.ds(t, 1), :] = jnp.sum(total, axis=0, keepdims=True)

        copies = []
        for d in range(1, mem_count):
            copies.append(
                pltpu.make_async_remote_copy(
                    src_ref=part.at[step],
                    dst_ref=peers.at[step, d - 1],
                    send_sem=peer_send.at[step, d - 1],
                    recv_sem=peer_recv.at[step, d - 1],
                    device_id={"mem": lax.rem(me_mem + d, mem_count)},
                    device_id_type=MESH,
                )
            )
            copies[-1].start()
        for copy in copies:
            copy.wait_recv()
        for r in range(rows):
            total = part[step, r]
            for d in range(1, mem_count):
                total = total + peers[step, d - 1, r]
            coarse[step, r] = total

        def rim_copy(side):
            return to_side(
                side,
                coarse.at[step, 0 if side == 0 else rows - 1],
                rim.at[step, 1 - side],
                rim_send.at[step, side],
                rim_recv.at[step, 1 - side],
            )

        for side in range(2):

            @pl.when(has[side])
            def _():
                rim_copy(side).start()

        def interpolate(line_of, values, first):
            doubled = jnp.concatenate([values, values], axis=0)
            moved = [rolled(doubled, -shift) for shift in range(-REACH, REACH + 1)]
            for r in range(rows):
                if abs(line_of - r) > 1:
                    continue
                for p in range(2):
                    total = None
                    for col in range(COLS):
                        term = planes[(line_of - r + 1) * COLS + col, r, p] * moved[col]
                        total = term if total is None else total + term
                    if r in first:
                        fine[r, p] = fine[r, p] + total
                    else:
                        fine[r, p] = total
                first.add(r)

        first = set()
        for r in range(rows):
            interpolate(r, coarse[step, r], first)
        for side in range(2):

            @pl.when(has[side])
            def _():
                rim_copy(1 - side).wait_recv()

        interpolate(-1, rim[step, 0], first)
        interpolate(rows, rim[step, 1], first)

        backs = []
        for r in range(rows):
            even, odd = stencil(fine[r, 0], fine[r, 1])
            even = mask[r, 0] * (even - target[r, 0])
            odd = mask[r, 1] * (odd - target[r, 1])
            backs.append(stencil(even, odd))
        for line_of in range(-1, rows + 1):
            landed = None
            for col in range(COLS):
                gathered = None
                for r in range(rows):
                    if abs(line_of - r) > 1:
                        continue
                    for p in range(2):
                        term = planes[(line_of - r + 1) * COLS + col, r, p] * backs[r][p]
                        gathered = term if gathered is None else gathered + term
                gathered = rolled(gathered, col - REACH)
                landed = gathered if landed is None else landed + gathered
            land[step, line_of + 1] = landed[:slots] + landed[slots:]

        def land_copy(side):
            return to_side(
                side,
                land.at[step, 0 if side == 0 else rows + 1],
                land_rim.at[step, 1 - side],
                land_send.at[step, side],
                land_recv.at[step, 1 - side],
            )

        for side in range(2):

            @pl.when(has[side])
            def _():
                land_copy(side).start()

        for side in range(2):

            @pl.when(has[side])
            def _():
                land_copy(1 - side).wait_recv()

        for r in range(rows):
            total = land[step, r + 1]
            if r == 0:
                total = total + land_rim[step, 0]
            if r == rows - 1:
                total = total + land_rim[step, 1]
            back[r] = total

        for g in range(groups):
            part_of = pl.ds(g * GROUP, GROUP)
            for r in range(rows):
                total = None
                for t in range(slots):
                    term = ens[t, r, part_of, :] * back[r, pl.ds(t, 1), :]
                    total = term if total is None else total + term
                edge[2 * step + 1, r, part_of, :] = total
            edge_start(2 * step + 1, g)
        for g in range(groups):
            part_of = pl.ds(g * GROUP, GROUP)
            edge_wait(2 * step + 1, g)
            spreads = spread(2 * step + 1, g)
            for r in range(rows):
                before = now[r, part_of, :]
                after = before - STEP_SIZE * (before + lon_filter(spreads[r], weights[r]))
                if step < GRAD_STEPS - 1:
                    now[r, part_of, :] = after
                    edge[2 * step + 2, r, part_of, :] = lon_filter(after, weights[r])
                else:
                    result[r, part_of, :] = after
            if step < GRAD_STEPS - 1:
                edge_start(2 * step + 2, g)

        for copy in copies:
            copy.wait_send()
        for side in range(2):

            @pl.when(has[side])
            def _():
                rim_copy(side).wait_send()
                land_copy(side).wait_send()

    stores = []
    for r in range(rows):
        stores.append(pltpu.make_async_copy(result.at[r], out.at[:, r, :], load_sem.at[r]))
        stores[-1].start()
    for phase in range(2 * GRAD_STEPS):
        edge_done(phase)
    for store in stores:
        store.wait()


def local(control, ensemble, widths, source, weight, obs_mask, innovation):
    members, slots, rows, lon = ensemble.shape
    mem_count, lat_count = lax.axis_size("mem"), lax.axis_size("lat")
    phases = 2 * GRAD_STEPS
    fine_rows = 2 * rows
    f32 = jnp.float32
    vmem = pl.BlockSpec(memory_space=pltpu.VMEM)
    anywhere = pl.BlockSpec(memory_space=pl.ANY)
    groups = members // GROUP
    stacked = 2 * source.shape[0] * fine_rows + 2 * slots * fine_rows
    dma = pltpu.SemaphoreType.DMA
    return pl.pallas_call(
        functools.partial(kernel, (slots, members, rows, lon, mem_count, lat_count)),
        out_shape=jax.ShapeDtypeStruct(control.shape, f32),
        in_specs=[
            pl.BlockSpec(memory_space=pltpu.SMEM),
            anywhere,
            anywhere,
            vmem,
            vmem,
            vmem,
            vmem,
        ],
        out_specs=anywhere,
        scratch_shapes=[
            pltpu.VMEM((slots, rows, members, lon), f32),
            pltpu.VMEM((rows, members, lon), f32),
            pltpu.VMEM((phases, rows, members, lon), f32),
            pltpu.VMEM((phases, 2, members, lon), f32),
            pltpu.VMEM((rows, members, lon), f32),
            pltpu.VMEM((rows, members, lon), f32),
            pltpu.VMEM((stacked, 2 * lon), f32),
            pltpu.VMEM((2, stacked, lon), f32),
            pltpu.VMEM((3 * COLS, rows, 2, 2 * slots, lon), f32),
            pltpu.VMEM((rows, 2, 2 * slots, lon), f32),
            pltpu.VMEM((rows, 2, 2 * slots, lon), f32),
            pltpu.VMEM((rows, 2, 2 * slots, lon), f32),
            pltpu.VMEM((GRAD_STEPS, rows, slots, lon), f32),
            pltpu.VMEM((GRAD_STEPS, mem_count - 1, rows, slots, lon), f32),
            pltpu.VMEM((GRAD_STEPS, rows, slots, lon), f32),
            pltpu.VMEM((GRAD_STEPS, 2, slots, lon), f32),
            pltpu.VMEM((GRAD_STEPS, rows + 2, slots, lon), f32),
            pltpu.VMEM((GRAD_STEPS, 2, slots, lon), f32),
            pltpu.VMEM((rows, slots, lon), f32),
            dma((rows + slots * rows,)),
            dma((phases, 2, groups)),
            dma((phases, 2, groups)),
            dma((GRAD_STEPS, mem_count - 1)),
            dma((GRAD_STEPS, mem_count - 1)),
            dma((GRAD_STEPS, 2)),
            dma((GRAD_STEPS, 2)),
            dma((GRAD_STEPS, 2)),
            dma((GRAD_STEPS, 2)),
        ],
        compiler_params=pltpu.CompilerParams(
            collective_id=0, has_side_effects=True, vmem_limit_bytes=48 * 1024 * 1024
        ),
    )(widths, control, ensemble, source, weight, obs_mask, innovation)


def solution(mesh):
    in_specs = (
        P("mem", "lat", None),
        P("mem", None, "lat", None),
        P("lat"),
        P(None, "lat", None),
        P(None, "lat", None),
        P(None, "lat", None),
        P(None, "lat", None),
    )
    out_specs = P("mem", "lat", None)
    return jax.shard_map(local, mesh=mesh, in_specs=in_specs, out_specs=out_specs, check_vma=False)
```

time: 420 us -> 59.4 us (0.14)
  the two profiles are of different devices: /device:TPU:0 before, /device:TPU:12 now
where the time goes in v1:
time: 59.4 us; the launch traced here: 59.1 us
  Pallas kernels  52 us (88%)
  local copies, waits for them, and re-layouts  7.15 us (12%)
    pallas_call x1, Pallas kernels, local(): pl.pallas_call(functools.partial(kernel, (slots, members, rows, lon, mem_...  52 us
    unnamed x15, local copies, waits for them, and re-layouts  7.15 us

profile of v1, /device:TPU:12, one launch (start us, length us, event | category | flops | bytes accessed | tf_op | source)
XLA Modules:
  0.0 59.1 jit_solution(14308371917630668807)
XLA Ops:
  0.0 0.0 copy-start
  0.0 1.2 %copy-done = f32[32,4,2,1024]{3,2,1,0:T(2,128)S(1)} copy-done((f32[32,4,2,1024]{3,2,1,0:T(2,128)S(1)}, f32[32,4,2,1024]{3,2,1,0:T(2,128)}, u32[]{:S(2)}) %copy-start) | copy-done | bytes 1048600
  1.2 0.0 copy-start.1
  1.2 0.9 %copy-done.1 = f32[32,2,1024]{2,1,0:T(2,128)S(1)} copy-done((f32[32,2,1024]{2,1,0:T(2,128)S(1)}, f32[32,2,1024]{2,1,0:T(2,128)}, u32[]{:S(2)}) %copy-start.1) | copy-done | bytes 262168
  2.2 0.0 copy-start.2
  2.2 0.9 %copy-done.2 = s32[4,4,2048]{2,1,0:T(4,128)S(1)} copy-done((s32[4,4,2048]{2,1,0:T(4,128)S(1)}, s32[4,4,2048]{2,1,0:T(4,128)}, u32[]{:S(2)}) %copy-start.2) | copy-done | bytes 131096
  3.1 0.0 copy-start.3
  3.1 0.9 %copy-done.3 = f32[4,4,2048]{2,1,0:T(4,128)S(1)} copy-done((f32[4,4,2048]{2,1,0:T(4,128)S(1)}, f32[4,4,2048]{2,1,0:T(4,128)}, u32[]{:S(2)}) %copy-start.3) | copy-done | bytes 131096
  4.0 0.0 copy-start.4
  4.0 0.9 %copy-done.4 = s32[4,4,2048]{2,1,0:T(4,128)S(1)} copy-done((s32[4,4,2048]{2,1,0:T(4,128)S(1)}, s32[4,4,2048]{2,1,0:T(4,128)}, u32[]{:S(2)}) %copy-start.4) | copy-done | bytes 131096
  4.9 0.0 copy-start.5
  4.9 0.9 %copy-done.5 = f32[4,4,2048]{2,1,0:T(4,128)S(1)} copy-done((f32[4,4,2048]{2,1,0:T(4,128)S(1)}, f32[4,4,2048]{2,1,0:T(4,128)}, u32[]{:S(2)}) %copy-start.5) | copy-done | bytes 131096
  5.8 0.0 copy-start.6
  5.8 0.7 %copy-done.6 = s32[2]{0:T(128)S(1)} copy-done((s32[2]{0:T(128)S(1)}, s32[2]{0:T(128)}, u32[]{:S(2)}) %copy-start.6) | copy-done | bytes 32
  6.5 52.0 %shard_map.73 = f32[32,2,1024]{2,1,0:T(2,128)S(1)} custom-call(s32[2]{0:T(128)S(1)} %copy-done.6, f32[32,2,1024]{2,1,0:T(2,128)S(1)} %copy-done.1, f32[32,4,2,1024]{3,2,1,0:T(2,128)S(1)} %copy-done, s32[4,4,2048]{2,1,0:T(4,128)S(1)} %copy-done.2, f32[4,4,2048]{2,1,0:T(4,128)S(1)} %copy-done.3, s32[4,4,2048]{2,1,0:T(4,128)S(1)} %copy-done.4, ...), custom_call_target="tpu_custom_call" | custom-call | tf_op jit(solution)/shard_map/pallas_call | solution.py:438
  58.4 0.7 %copy.9 = f32[32,2,1024]{2,1,0:T(2,128)} copy(f32[32,2,1024]{2,1,0:T(2,128)S(1)} %shard_map.73) | data formatting | bytes 524288
Async XLA Ops:
  0.0 1.2 %copy-start = (f32[32,4,2,1024]{3,2,1,0:T(2,128)S(1)}, f32[32,4,2,1024]{3,2,1,0:T(2,128)}, u32[]{:S(2)}) copy-start(f32[32,4,2,1024]{3,2,1,0:T(2,128)} %ensemble.1) | copy-start | bytes 3145732
  1.2 0.9 %copy-start.1 = (f32[32,2,1024]{2,1,0:T(2,128)S(1)}, f32[32,2,1024]{2,1,0:T(2,128)}, u32[]{:S(2)}) copy-start(f32[32,2,1024]{2,1,0:T(2,128)} %control.1) | copy-start | bytes 786436
  2.2 0.9 %copy-start.2 = (s32[4,4,2048]{2,1,0:T(4,128)S(1)}, s32[4,4,2048]{2,1,0:T(4,128)}, u32[]{:S(2)}) copy-start(s32[4,4,2048]{2,1,0:T(4,128)} %source.1) | copy-start | bytes 393220
  3.1 0.9 %copy-start.3 = (f32[4,4,2048]{2,1,0:T(4,128)S(1)}, f32[4,4,2048]{2,1,0:T(4,128)}, u32[]{:S(2)}) copy-start(f32[4,4,2048]{2,1,0:T(4,128)} %weight.1) | copy-start | bytes 393220
  4.0 0.9 %copy-start.4 = (s32[4,4,2048]{2,1,0:T(4,128)S(1)}, s32[4,4,2048]{2,1,0:T(4,128)}, u32[]{:S(2)}) copy-start(s32[4,4,2048]{2,1,0:T(4,128)} %obs_mask.1) | copy-start | bytes 393220
  4.9 0.9 %copy-start.5 = (f32[4,4,2048]{2,1,0:T(4,128)S(1)}, f32[4,4,2048]{2,1,0:T(4,128)}, u32[]{:S(2)}) copy-start(f32[4,4,2048]{2,1,0:T(4,128)} %innovation.1) | copy-start | bytes 393220
  5.8 0.7 %copy-start.6 = (s32[2]{0:T(128)S(1)}, s32[2]{0:T(128)}, u32[]{:S(2)}) copy-start(s32[2]{0:T(128)} %widths.1) | copy-start | bytes 28

commit v2 on v1

--- a/solution.py
+++ b/solution.py
@@ -40,14 +40,19 @@
 
 def kernel(
     sizes,
-    widths,
+    widths_far,
     control,
     ensemble,
+    source_far,
+    weight_far,
+    obs_mask_far,
+    innovation_far,
+    out,
+    widths,
     source,
     weight,
     obs_mask,
     innovation,
-    out,
     ens,
     now,
     edge,
@@ -68,6 +73,7 @@
     land_rim,
     back,
     load_sem,
+    store_sem,
     edge_send,
     edge_recv,
     peer_send,
@@ -85,16 +91,21 @@
     beside = (me_lat - 1, me_lat + 1)
 
     loads = []
+
+    def load(src, dst):
+        loads.append(pltpu.make_async_copy(src, dst, load_sem.at[len(loads)]))
+        loads[-1].start()
+
+    load(widths_far, widths)
     for r in range(rows):
-        loads.append(pltpu.make_async_copy(control.at[:, r, :], now.at[r], load_sem.at[r]))
-        loads[-1].start()
+        load(control.at[:, r, :], now.at[r])
+    load(source_far, source)
+    load(weight_far, weight)
+    load(obs_mask_far, obs_mask)
+    load(innovation_far, innovation)
     for t in range(slots):
         for r in range(rows):
-            number = rows + t * rows + r
-            loads.append(
-                pltpu.make_async_copy(ensemble.at[:, t, r, :], ens.at[t, r], load_sem.at[number])
-            )
-            loads[-1].start()
+            load(ensemble.at[:, t, r, :], ens.at[t, r])
 
     barrier = pltpu.get_barrier_semaphore()
     for d in range(1, mem_count):
@@ -159,6 +170,7 @@
                 def _():
                     edge_copy(phase, side, g).wait_send()
 
+    loads[0].wait()
     weights = []
     for r in range(rows):
         width = widths[r]
@@ -188,13 +200,16 @@
                 land_rim[step, side] = jnp.zeros((slots, lon), jnp.float32)
 
     for r in range(rows):
-        loads[r].wait()
+        loads[1 + r].wait()
     for g in range(groups):
         part_of = pl.ds(g * GROUP, GROUP)
         for r in range(rows):
             edge[0, r, part_of, :] = lon_filter(now[r, part_of, :], weights[r])
         edge_start(0, g)
 
+    early = 1 + rows + 4
+    for copy in loads[1 + rows : early]:
+        copy.wait()
     fine_rows = 2 * rows
     four = source.shape[0]
     for s in range(four):
@@ -250,9 +265,10 @@
                     total = total + jnp.where(codes[s] == number, heavy[s], 0.0)
                 planes[number, r, p] = total
 
-    for load in loads[rows:]:
-        load.wait()
-
+    for copy in loads[early:]:
+        copy.wait()
+
+    stores = []
     for step in range(GRAD_STEPS):
         for g in range(groups):
             edge_wait(2 * step, g)
@@ -402,6 +418,12 @@
                     edge[2 * step + 2, r, part_of, :] = lon_filter(after, weights[r])
                 else:
                     result[r, part_of, :] = after
+                    stores.append(
+                        pltpu.make_async_copy(
+                            result.at[r, part_of], out.at[part_of, r, :], store_sem.at[r, g]
+                        )
+                    )
+                    stores[-1].start()
             if step < GRAD_STEPS - 1:
                 edge_start(2 * step + 2, g)
 
@@ -414,10 +436,6 @@
                 rim_copy(side).wait_send()
                 land_copy(side).wait_send()
 
-    stores = []
-    for r in range(rows):
-        stores.append(pltpu.make_async_copy(result.at[r], out.at[:, r, :], load_sem.at[r]))
-        stores[-1].start()
     for phase in range(2 * GRAD_STEPS):
         edge_done(phase)
     for store in stores:
@@ -430,25 +448,21 @@
     phases = 2 * GRAD_STEPS
     fine_rows = 2 * rows
     f32 = jnp.float32
-    vmem = pl.BlockSpec(memory_space=pltpu.VMEM)
-    anywhere = pl.BlockSpec(memory_space=pl.ANY)
+    hbm = pl.BlockSpec(memory_space=pltpu.HBM)
     groups = members // GROUP
     stacked = 2 * source.shape[0] * fine_rows + 2 * slots * fine_rows
     dma = pltpu.SemaphoreType.DMA
     return pl.pallas_call(
         functools.partial(kernel, (slots, members, rows, lon, mem_count, lat_count)),
         out_shape=jax.ShapeDtypeStruct(control.shape, f32),
-        in_specs=[
-            pl.BlockSpec(memory_space=pltpu.SMEM),
-            anywhere,
-            anywhere,
-            vmem,
-            vmem,
-            vmem,
-            vmem,
-        ],
-        out_specs=anywhere,
+        in_specs=[hbm] * 7,
+        out_specs=hbm,
         scratch_shapes=[
+            pltpu.SMEM(widths.shape, jnp.int32),
+            pltpu.VMEM(source.shape, jnp.int32),
+            pltpu.VMEM(weight.shape, f32),
+            pltpu.VMEM(obs_mask.shape, jnp.int32),
+            pltpu.VMEM(innovation.shape, f32),
             pltpu.VMEM((slots, rows, members, lon), f32),
             pltpu.VMEM((rows, members, lon), f32),
             pltpu.VMEM((phases, rows, members, lon), f32),
@@ -468,7 +482,8 @@
             pltpu.VMEM((GRAD_STEPS, rows + 2, slots, lon), f32),
             pltpu.VMEM((GRAD_STEPS, 2, slots, lon), f32),
             pltpu.VMEM((rows, slots, lon), f32),
-            dma((rows + slots * rows,)),
+            dma((5 + rows + slots * rows,)),
+            dma((rows, groups)),
             dma((phases, 2, groups)),
             dma((phases, 2, groups)),
             dma((GRAD_STEPS, mem_count - 1)),
@@ -479,7 +494,7 @@
             dma((GRAD_STEPS, 2)),
         ],
         compiler_params=pltpu.CompilerParams(
-            collective_id=0, has_side_effects=True, vmem_limit_bytes=48 * 1024 * 1024
+            collective_id=0, has_side_effects=True, vmem_limit_bytes=67043328
         ),
     )(widths, control, ensemble, source, weight, obs_mask, innovation)
 

time: 59.4 us -> 52.9 us (0.89)
  local copies, waits for them, and re-layouts: 7.15 us -> 1.67 us
  Pallas kernels: 52 us -> 51.1 us
    unnamed x15 -> x1, local copies, waits for them, and re-layouts: 7.15 us -> 1.67 us
    pallas_call x1, Pallas kernels: 52 us -> 51.1 us  [local(): pl.pallas_call(functools.partial(kernel, (slots, members, rows, lon, mem_...]
where the time goes in v2:
time: 52.9 us; the launch traced here: 52.7 us
  Pallas kernels  51.1 us (97%)
  local copies, waits for them, and re-layouts  1.67 us (3%)
    pallas_call x1, Pallas kernels, local(): pl.pallas_call(functools.partial(kernel, (slots, members, rows, lon, mem_...  51.1 us
    unnamed x1, local copies, waits for them, and re-layouts  1.67 us

profile of v2, /device:TPU:12, one launch (start us, length us, event | category | flops | bytes accessed | tf_op | source)
XLA Modules:
  0.0 52.7 jit_solution(1506874495189292956)
XLA Ops:
  0.0 51.1 %shard_map.73 = f32[32,2,1024]{2,1,0:T(2,128)} custom-call(s32[2]{0:T(128)} %widths_far.1, f32[32,2,1024]{2,1,0:T(2,128)} %control.1, f32[32,4,2,1024]{3,2,1,0:T(2,128)} %ensemble.1, s32[4,4,2048]{2,1,0:T(4,128)} %source_far.1, f32[4,4,2048]{2,1,0:T(4,128)} %weight_far.1, s32[4,4,2048]{2,1,0:T(4,128)} %obs_mask_far.1, f32[4,4,2048]{2,1,0:T(4,128)} %innovation_far.1), custom_call_target="tpu_custom_call" | custom-call | tf_op jit(solution)/shard_map/pallas_call | solution.py:455
  51.1 1.7 %copy.9 = f32[32,2,1024]{2,1,0:T(2,128)} copy(f32[32,2,1024]{2,1,0:T(2,128)} %shard_map.73) | data formatting | bytes 524288

commit v3 on v2

v3 whole, which is shorter than its diff:
```python
import functools

import jax
import jax.numpy as jnp
from jax import lax
from jax.experimental import pallas as pl
from jax.experimental.pallas import tpu as pltpu
from jax.sharding import PartitionSpec as P

WIDEST = 4
GRAD_STEPS = 2
C_MID = 0.5
C_SIDE = 0.25
STEP_SIZE = 0.5
GROUP = 8
LANES = 128
REACH = 2
COLS = 2 * REACH + 1
MESH = pl.DeviceIdType.MESH


def rolled(x, shift):
    shift = shift % x.shape[-1]
    return x if shift == 0 else pltpu.roll(x, shift, x.ndim - 1)


def lon_filter(x, weights):
    total = x * weights[0]
    for k in range(1, WIDEST + 1):
        total = total + (rolled(x, k) + rolled(x, -k)) * weights[k]
    return total


def stencil(even, odd):
    return (
        0.25 * (rolled(odd, 1) + odd) + 0.5 * even,
        0.25 * (even + rolled(even, -1)) + 0.5 * odd,
    )


def kernel(
    sizes,
    widths_far,
    control,
    ensemble,
    source_far,
    weight_far,
    obs_mask_far,
    innovation_far,
    out,
    widths,
    source,
    weight,
    obs_mask,
    innovation,
    ens,
    now,
    edge,
    halo,
    forward,
    result,
    rows_in,
    rows_out,
    planes,
    mask,
    target,
    part,
    peers,
    rim,
    land,
    land_peers,
    land_rim,
    back,
    load_sem,
    store_sem,
    edge_send,
    edge_recv,
    peer_send,
    peer_recv,
    rim_send,
    rim_recv,
    land_send,
    land_recv,
    land_rim_send,
    land_rim_recv,
):
    slots, members, rows, lon, mem_count, lat_count = sizes
    groups = members // GROUP
    share = slots // mem_count
    fine_rows = 2 * rows
    me_mem = lax.axis_index("mem")
    me_lat = lax.axis_index("lat")
    has = (me_lat > 0, me_lat < lat_count - 1)
    beside = (me_lat - 1, me_lat + 1)

    loads = []

    def load(src, dst):
        loads.append(pltpu.make_async_copy(src, dst, load_sem.at[len(loads)]))
        loads[-1].start()

    load(widths_far, widths)
    for r in range(rows):
        load(control.at[:, r, :], now.at[r])
    load(source_far, source)
    load(weight_far, weight)
    own_slots = pl.ds(me_mem * share, share)
    load(obs_mask_far.at[own_slots], obs_mask)
    load(innovation_far.at[own_slots], innovation)
    for t in range(slots):
        for r in range(rows):
            load(ensemble.at[:, t, r, :], ens.at[t, r])

    mates = [lax.rem(me_mem + d, mem_count) for d in range(mem_count)]
    barrier = pltpu.get_barrier_semaphore()
    for d in range(1, mem_count):
        pl.semaphore_signal(barrier, inc=1, device_id={"mem": mates[d]}, device_id_type=MESH)
    for side in range(2):

        @pl.when(has[side])
        def _():
            for d in range(mem_count):
                pl.semaphore_signal(
                    barrier,
                    inc=1,
                    device_id={"mem": mates[d], "lat": beside[side]},
                    device_id_type=MESH,
                )

    sides = has[0].astype(jnp.int32) + has[1].astype(jnp.int32)
    pl.semaphore_wait(barrier, mem_count - 1 + mem_count * sides)

    def send_to(where, src, dst, send, recv):
        return pltpu.make_async_remote_copy(
            src_ref=src,
            dst_ref=dst,
            send_sem=send,
            recv_sem=recv,
            device_id=where,
            device_id_type=MESH,
        )

    def edge_copy(phase, side, g):
        row = 0 if side == 0 else rows - 1
        part_of = pl.ds(g * GROUP, GROUP)
        return send_to(
            {"lat": beside[side]},
            edge.at[phase, row, part_of],
            halo.at[phase, 1 - side, part_of],
            edge_send.at[phase, side, g],
            edge_recv.at[phase, 1 - side, g],
        )

    def edge_start(phase, g):
        for side in range(2):

            @pl.when(has[side])
            def _():
                edge_copy(phase, side, g).start()

    def edge_wait(phase, g):
        for side in range(2):

            @pl.when(has[side])
            def _():
                edge_copy(phase, 1 - side, g).wait_recv()

    def edge_done(phase):
        for g in range(groups):
            for side in range(2):

                @pl.when(has[side])
                def _():
                    edge_copy(phase, side, g).wait_send()

    loads[0].wait()
    weights = []
    for r in range(rows):
        width = widths[r]
        scale = jnp.float32(1.0 / (2 * WIDEST + 1))
        for w in range(WIDEST):
            scale = jnp.where(width == w, jnp.float32(1.0 / (2 * w + 1)), scale)
        weights.append(
            [jnp.where(width >= k, scale, jnp.float32(0.0)) for k in range(WIDEST + 1)]
        )

    def spread(phase, g):
        part_of = pl.ds(g * GROUP, GROUP)
        own = [edge[phase, r, part_of, :] for r in range(rows)]
        padded = [halo[phase, 0, part_of, :], *own, halo[phase, 1, part_of, :]]
        return [
            C_MID * padded[r + 1] + C_SIDE * (padded[r] + padded[r + 2]) for r in range(rows)
        ]

    for side in range(2):

        @pl.when(jnp.logical_not(has[side]))
        def _():
            for phase in range(2 * GRAD_STEPS):
                halo[phase, side] = jnp.zeros((members, lon), jnp.float32)
            for step in range(GRAD_STEPS):
                for d in range(mem_count):
                    rim[step, side, d] = jnp.zeros((share, lon), jnp.float32)
                    land_rim[step, side, d] = jnp.zeros((share, lon), jnp.float32)

    for r in range(rows):
        loads[1 + r].wait()
    for g in range(groups):
        part_of = pl.ds(g * GROUP, GROUP)
        for r in range(rows):
            edge[0, r, part_of, :] = lon_filter(now[r, part_of, :], weights[r])
        edge_start(0, g)

    early = 1 + rows + 4
    for copy in loads[1 + rows : early]:
        copy.wait()
    four = source.shape[0]
    for s in range(four):
        rows_in[pl.ds(s * fine_rows, fine_rows), :] = source[s].astype(jnp.float32)
        rows_in[pl.ds((four + s) * fine_rows, fine_rows), :] = weight[s]
    for s in range(share):
        top = (2 * four + s) * fine_rows
        rows_in[pl.ds(top, fine_rows), :] = obs_mask[s].astype(jnp.float32)
        rows_in[pl.ds(top + share * fine_rows, fine_rows), :] = innovation[s]
    line = lax.broadcasted_iota(jnp.int32, (2 * LANES, 2 * LANES), 0)
    column = lax.broadcasted_iota(jnp.int32, (2 * LANES, 2 * LANES), 1)
    wanted = jnp.where(column < LANES, 2 * column, 2 * (column - LANES) + 1)
    pick = jnp.where(line == wanted, 1.0, 0.0).astype(jnp.float32)
    for block in range(lon // LANES):
        both = jnp.dot(
            rows_in[:, pl.ds(block * 2 * LANES, 2 * LANES)],
            pick,
            precision=lax.Precision.HIGHEST,
            preferred_element_type=jnp.float32,
        )
        rows_out[0, :, pl.ds(block * LANES, LANES)] = both[:, :LANES]
        rows_out[1, :, pl.ds(block * LANES, LANES)] = both[:, LANES:]

    def both_parities(number):
        span = pl.ds(number * fine_rows, fine_rows)
        return jnp.concatenate([rows_out[0, span, :], rows_out[1, span, :]], axis=0)

    shape = (2 * fine_rows, lon)
    across = lax.broadcasted_iota(jnp.int32, shape, 1).astype(jnp.float32)
    down = lax.broadcasted_iota(jnp.int32, shape, 0).astype(jnp.float32)
    down = down - fine_rows * jnp.floor((down + 0.5) * (1.0 / fine_rows))
    parent = jnp.floor((down + 0.5) * 0.5)
    codes = []
    for s in range(four):
        flat = jnp.floor(both_parities(s) + 0.5)
        line_of = jnp.floor((flat + 0.5) * (1.0 / lon))
        shift = flat - line_of * lon - across + REACH
        shift = jnp.where(shift < 0.0, shift + lon, shift)
        shift = jnp.where(shift >= lon, shift - lon, shift)
        codes.append((line_of - parent) * COLS + shift)
    for number in range(3 * COLS):
        total = None
        for s in range(four):
            term = jnp.where(codes[s] == number, both_parities(four + s), 0.0)
            total = term if total is None else total + term
        planes[number] = total
    for s in range(share):
        mask[s] = both_parities(2 * four + s)
        target[s] = both_parities(2 * four + share + s)

    for copy in loads[early:]:
        copy.wait()

    stores = []
    for step in range(GRAD_STEPS):
        for g in range(groups):
            edge_wait(2 * step, g)
            spreads = spread(2 * step, g)
            for r in range(rows):
                forward[r, pl.ds(g * GROUP, GROUP), :] = spreads[r]
        for r in range(rows):
            for t in range(slots):
                total = jnp.zeros((GROUP, lon), jnp.float32)
                for g in range(groups):
                    part_of = pl.ds(g * GROUP, GROUP)
                    total = total + ens[t, r, part_of, :] * forward[r, part_of, :]
                total = jnp.sum(total, axis=0, keepdims=True)
                part[step, t // share, r, pl.ds(t % share, 1), :] = total

        def peer_copy(d):
            return send_to(
                {"mem": mates[d]},
                part.at[step, mates[d]],
                peers.at[step, d - 1],
                peer_send.at[step, d - 1],
                peer_recv.at[step, d - 1],
            )

        def rim_copy(side, d):
            return send_to(
                {"mem": mates[d], "lat": beside[side]},
                part.at[step, mates[d], 0 if side == 0 else rows - 1],
                rim.at[step, 1 - side, d],
                rim_send.at[step, side, d],
                rim_recv.at[step, 1 - side, d],
            )

        def land_copy(d):
            return send_to(
                {"mem": mates[d]},
                land.at[step, pl.ds(1, rows)],
                land_peers.at[step, d - 1],
                land_send.at[step, d - 1],
                land_recv.at[step, d - 1],
            )

        def land_rim_copy(side, d):
            return send_to(
                {"mem": mates[d], "lat": beside[side]},
                land.at[step, 0 if side == 0 else rows + 1],
                land_rim.at[step, 1 - side, d],
                land_rim_send.at[step, side, d],
                land_rim_recv.at[step, 1 - side, d],
            )

        def exchange(near, far):
            for side in range(2):

                @pl.when(has[side])
                def _():
                    for d in range(mem_count):
                        far(side, d).start()

            for d in range(1, mem_count):
                near(d).start()
            for d in range(1, mem_count):
                near(d).wait_recv()
            for side in range(2):

                @pl.when(has[side])
                def _():
                    for d in range(mem_count):
                        far(1 - side, d).wait_recv()

        def exchange_done(near, far):
            for d in range(1, mem_count):
                near(d).wait_send()
            for side in range(2):

                @pl.when(has[side])
                def _():
                    for d in range(mem_count):
                        far(side, d).wait_send()

        exchange(peer_copy, rim_copy)
        for s in range(share):
            lines = []
            for r in range(-1, rows + 1):
                if r < 0 or r == rows:
                    side = 0 if r < 0 else 1
                    total = rim[step, side, 0, pl.ds(s, 1), :]
                    for d in range(1, mem_count):
                        total = total + rim[step, side, d, pl.ds(s, 1), :]
                else:
                    total = part[step, me_mem, r, pl.ds(s, 1), :]
                    for d in range(1, mem_count):
                        total = total + peers[step, d - 1, r, pl.ds(s, 1), :]
                lines.append(total)
            total = None
            for near in range(3):
                stack = [
                    jnp.broadcast_to(lines[r + near], (2, lon)) for r in range(rows)
                ]
                stack = jnp.concatenate(stack * 2, axis=0)
                for col in range(COLS):
                    term = planes[near * COLS + col] * rolled(stack, REACH - col)
                    total = term if total is None else total + term
            even, odd = stencil(total[:fine_rows], total[fine_rows:])
            even = mask[s, :fine_rows, :] * (even - target[s, :fine_rows, :])
            odd = mask[s, fine_rows:, :] * (odd - target[s, fine_rows:, :])
            returned = jnp.concatenate(stencil(even, odd), axis=0)
            landed = [None] * (rows + 2)
            for near in range(3):
                total = None
                for col in range(COLS):
                    term = rolled(planes[near * COLS + col] * returned, col - REACH)
                    total = term if total is None else total + term
                total = total[:fine_rows] + total[fine_rows:]
                for r in range(rows):
                    term = total[2 * r : 2 * r + 1] + total[2 * r + 1 : 2 * r + 2]
                    before = landed[r + near]
                    landed[r + near] = term if before is None else before + term
            for r in range(rows + 2):
                land[step, r, pl.ds(s, 1), :] = landed[r]

        exchange(land_copy, land_rim_copy)
        for d in range(mem_count):
            for s in range(share):
                one = pl.ds(s, 1)
                for r in range(rows):
                    if d == 0:
                        total = land[step, r + 1, one, :]
                    else:
                        total = land_peers[step, d - 1, r, one, :]
                    if r == 0:
                        total = total + land_rim[step, 0, d, one, :]
                    if r == rows - 1:
                        total = total + land_rim[step, 1, d, one, :]
                    back[r, pl.ds(d * share + s, 1), :] = total

        slot_of = []
        for d in range(mem_count):
            owner = lax.rem(me_mem + mem_count - d, mem_count)
            slot_of.extend(owner * share + s for s in range(share))
        for g in range(groups):
            part_of = pl.ds(g * GROUP, GROUP)
            for r in range(rows):
                total = None
                for t in range(slots):
                    term = ens[slot_of[t], r, part_of, :] * back[r, pl.ds(t, 1), :]
                    total = term if total is None else total + term
                edge[2 * step + 1, r, part_of, :] = total
            edge_start(2 * step + 1, g)
        for g in range(groups):
            part_of = pl.ds(g * GROUP, GROUP)
            edge_wait(2 * step + 1, g)
            spreads = spread(2 * step + 1, g)
            for r in range(rows):
                before = now[r, part_of, :]
                after = before - STEP_SIZE * (before + lon_filter(spreads[r], weights[r]))
                if step < GRAD_STEPS - 1:
                    now[r, part_of, :] = after
                    edge[2 * step + 2, r, part_of, :] = lon_filter(after, weights[r])
                else:
                    result[r, part_of, :] = after
                    stores.append(
                        pltpu.make_async_copy(
                            result.at[r, part_of], out.at[part_of, r, :], store_sem.at[r, g]
                        )
                    )
                    stores[-1].start()
            if step < GRAD_STEPS - 1:
                edge_start(2 * step + 2, g)

        exchange_done(peer_copy, rim_copy)
        exchange_done(land_copy, land_rim_copy)

    for phase in range(2 * GRAD_STEPS):
        edge_done(phase)
    for store in stores:
        store.wait()


def local(control, ensemble, widths, source, weight, obs_mask, innovation):
    members, slots, rows, lon = ensemble.shape
    mem_count, lat_count = lax.axis_size("mem"), lax.axis_size("lat")
    phases = 2 * GRAD_STEPS
    fine_rows = 2 * rows
    share = slots // mem_count
    f32 = jnp.float32
    hbm = pl.BlockSpec(memory_space=pltpu.HBM)
    groups = members // GROUP
    stacked = 2 * source.shape[0] * fine_rows + 2 * share * fine_rows
    dma = pltpu.SemaphoreType.DMA
    return pl.pallas_call(
        functools.partial(kernel, (slots, members, rows, lon, mem_count, lat_count)),
        out_shape=jax.ShapeDtypeStruct(control.shape, f32),
        in_specs=[hbm] * 7,
        out_specs=hbm,
        scratch_shapes=[
            pltpu.SMEM(widths.shape, jnp.int32),
            pltpu.VMEM(source.shape, jnp.int32),
            pltpu.VMEM(weight.shape, f32),
            pltpu.VMEM((share, *obs_mask.shape[1:]), jnp.int32),
            pltpu.VMEM((share, *innovation.shape[1:]), f32),
            pltpu.VMEM((slots, rows, members, lon), f32),
            pltpu.VMEM((rows, members, lon), f32),
            pltpu.VMEM((phases, rows, members, lon), f32),
            pltpu.VMEM((phases, 2, members, lon), f32),
            pltpu.VMEM((rows, members, lon), f32),
            pltpu.VMEM((rows, members, lon), f32),
            pltpu.VMEM((stacked, 2 * lon), f32),
            pltpu.VMEM((2, stacked, lon), f32),
            pltpu.VMEM((3 * COLS, 2 * fine_rows, lon), f32),
            pltpu.VMEM((share, 2 * fine_rows, lon), f32),
            pltpu.VMEM((share, 2 * fine_rows, lon), f32),
            pltpu.VMEM((GRAD_STEPS, mem_count, rows, share, lon), f32),
            pltpu.VMEM((GRAD_STEPS, mem_count - 1, rows, share, lon), f32),
            pltpu.VMEM((GRAD_STEPS, 2, mem_count, share, lon), f32),
            pltpu.VMEM((GRAD_STEPS, rows + 2, share, lon), f32),
            pltpu.VMEM((GRAD_STEPS, mem_count - 1, rows, share, lon), f32),
            pltpu.VMEM((GRAD_STEPS, 2, mem_count, share, lon), f32),
            pltpu.VMEM((rows, slots, lon), f32),
            dma((5 + rows + slots * rows,)),
            dma((rows, groups)),
            dma((phases, 2, groups)),
            dma((phases, 2, groups)),
            dma((GRAD_STEPS, mem_count - 1)),
            dma((GRAD_STEPS, mem_count - 1)),
            dma((GRAD_STEPS, 2, mem_count)),
            dma((GRAD_STEPS, 2, mem_count)),
            dma((GRAD_STEPS, mem_count - 1)),
            dma((GRAD_STEPS, mem_count - 1)),
            dma((GRAD_STEPS, 2, mem_count)),
            dma((GRAD_STEPS, 2, mem_count)),
        ],
        compiler_params=pltpu.CompilerParams(
            collective_id=0, has_side_effects=True, vmem_limit_bytes=67043328
        ),
    )(widths, control, ensemble, source, weight, obs_mask, innovation)


def solution(mesh):
    in_specs = (
        P("mem", "lat", None),
        P("mem", None, "lat", None),
        P("lat"),
        P(None, "lat", None),
        P(None, "lat", None),
        P(None, "lat", None),
        P(None, "lat", None),
    )
    out_specs = P("mem", "lat", None)
    return jax.shard_map(local, mesh=mesh, in_specs=in_specs, out_specs=out_specs, check_vma=False)
```

time: 52.9 us -> 52.1 us (0.985); the launches traced: 52.7 us -> 51.2 us
  Pallas kernels: 51.1 us -> 49.5 us
    pallas_call x1, Pallas kernels: 51.1 us -> 49.5 us  [local(): pl.pallas_call(functools.partial(kernel, (slots, members, rows, lon, mem_...]
where the time goes in v3:
time: 52.1 us; the launch traced here: 51.2 us
  Pallas kernels  49.5 us (95%)
  local copies, waits for them, and re-layouts  1.67 us (3%)
    pallas_call x1, Pallas kernels, local(): pl.pallas_call(functools.partial(kernel, (slots, members, rows, lon, mem_...  49.5 us
    unnamed x1, local copies, waits for them, and re-layouts  1.67 us

profile of v3, /device:TPU:12, one launch (start us, length us, event | category | flops | bytes accessed | tf_op | source)
XLA Modules:
  0.0 51.2 jit_solution(2061583693130935019)
XLA Ops:
  0.0 49.5 %shard_map.73 = f32[32,2,1024]{2,1,0:T(2,128)} custom-call(s32[2]{0:T(128)} %widths_far.1, f32[32,2,1024]{2,1,0:T(2,128)} %control.1, f32[32,4,2,1024]{3,2,1,0:T(2,128)} %ensemble.1, s32[4,4,2048]{2,1,0:T(4,128)} %source_far.1, f32[4,4,2048]{2,1,0:T(4,128)} %weight_far.1, s32[4,4,2048]{2,1,0:T(4,128)} %obs_mask_far.1, f32[4,4,2048]{2,1,0:T(4,128)} %innovation_far.1), custom_call_target="tpu_custom_call" | custom-call | tf_op jit(solution)/shard_map/pallas_call | solution.py:460
  49.5 1.7 %copy.9 = f32[32,2,1024]{2,1,0:T(2,128)} copy(f32[32,2,1024]{2,1,0:T(2,128)} %shard_map.73) | data formatting | bytes 524288

commit v4 on v3

--- a/solution.py
+++ b/solution.py
@@ -57,7 +57,7 @@
     now,
     edge,
     halo,
-    forward,
+    sums,
     result,
     rows_in,
     rows_out,
@@ -100,8 +100,10 @@
         loads[-1].start()
 
     load(widths_far, widths)
-    for r in range(rows):
-        load(control.at[:, r, :], now.at[r])
+    for g in range(groups):
+        for r in range(rows):
+            part_of = pl.ds(g * GROUP, GROUP)
+            load(control.at[part_of, r, :], now.at[r, part_of])
     load(source_far, source)
     load(weight_far, weight)
     own_slots = pl.ds(me_mem * share, share)
@@ -203,16 +205,15 @@
                     rim[step, side, d] = jnp.zeros((share, lon), jnp.float32)
                     land_rim[step, side, d] = jnp.zeros((share, lon), jnp.float32)
 
-    for r in range(rows):
-        loads[1 + r].wait()
     for g in range(groups):
         part_of = pl.ds(g * GROUP, GROUP)
         for r in range(rows):
+            loads[1 + g * rows + r].wait()
             edge[0, r, part_of, :] = lon_filter(now[r, part_of, :], weights[r])
         edge_start(0, g)
 
-    early = 1 + rows + 4
-    for copy in loads[1 + rows : early]:
+    early = 1 + groups * rows + 4
+    for copy in loads[early - 4 : early]:
         copy.wait()
     four = source.shape[0]
     for s in range(four):
@@ -271,15 +272,14 @@
         for g in range(groups):
             edge_wait(2 * step, g)
             spreads = spread(2 * step, g)
+            part_of = pl.ds(g * GROUP, GROUP)
             for r in range(rows):
-                forward[r, pl.ds(g * GROUP, GROUP), :] = spreads[r]
+                for t in range(slots):
+                    term = ens[t, r, part_of, :] * spreads[r]
+                    sums[r, t] = term if g == 0 else sums[r, t] + term
         for r in range(rows):
             for t in range(slots):
-                total = jnp.zeros((GROUP, lon), jnp.float32)
-                for g in range(groups):
-                    part_of = pl.ds(g * GROUP, GROUP)
-                    total = total + ens[t, r, part_of, :] * forward[r, part_of, :]
-                total = jnp.sum(total, axis=0, keepdims=True)
+                total = jnp.sum(sums[r, t], axis=0, keepdims=True)
                 part[step, t // share, r, pl.ds(t % share, 1), :] = total
 
         def peer_copy(d):
@@ -461,7 +461,7 @@
         functools.partial(kernel, (slots, members, rows, lon, mem_count, lat_count)),
         out_shape=jax.ShapeDtypeStruct(control.shape, f32),
         in_specs=[hbm] * 7,
-        out_specs=hbm,
+        out_specs=pl.BlockSpec(memory_space=pl.ANY),
         scratch_shapes=[
             pltpu.SMEM(widths.shape, jnp.int32),
             pltpu.VMEM(source.shape, jnp.int32),
@@ -472,7 +472,7 @@
             pltpu.VMEM((rows, members, lon), f32),
             pltpu.VMEM((phases, rows, members, lon), f32),
             pltpu.VMEM((phases, 2, members, lon), f32),
-            pltpu.VMEM((rows, members, lon), f32),
+            pltpu.VMEM((rows, slots, GROUP, lon), f32),
             pltpu.VMEM((rows, members, lon), f32),
             pltpu.VMEM((stacked, 2 * lon), f32),
             pltpu.VMEM((2, stacked, lon), f32),
@@ -486,7 +486,7 @@
             pltpu.VMEM((GRAD_STEPS, mem_count - 1, rows, share, lon), f32),
             pltpu.VMEM((GRAD_STEPS, 2, mem_count, share, lon), f32),
             pltpu.VMEM((rows, slots, lon), f32),
-            dma((5 + rows + slots * rows,)),
+            dma((5 + groups * rows + slots * rows,)),
             dma((rows, groups)),
             dma((phases, 2, groups)),
             dma((phases, 2, groups)),
@@ -500,9 +500,14 @@
             dma((GRAD_STEPS, 2, mem_count)),
         ],
         compiler_params=pltpu.CompilerParams(
-            collective_id=0, has_side_effects=True, vmem_limit_bytes=67043328
+            collective_id=0, has_side_effects=True, vmem_limit_bytes=48 * 1024 * 1024
         ),
-    )(widths, control, ensemble, source, weight, obs_mask, innovation)
+    )(
+        *[
+            pltpu.with_memory_space_constraint(x, pltpu.HBM)
+            for x in (widths, control, ensemble, source, weight, obs_mask, innovation)
+        ]
+    )
 
 
 def solution(mesh):

time: 52.1 us -> 50.8 us (0.975)
  local copies, waits for them, and re-layouts: 1.67 us -> 0.71 us
    unnamed x1, local copies, waits for them, and re-layouts: 1.67 us -> 0.71 us
where the time goes in v4:
time: 50.8 us; the launch traced here: 49.9 us
  Pallas kernels  49.2 us (97%)
  local copies, waits for them, and re-layouts  0.71 us (1%)
    pallas_call x1, Pallas kernels, local(): pl.pallas_call(functools.partial(kernel, (slots, members, rows, lon, mem_...  49.2 us

profile of v4, /device:TPU:12, one launch (start us, length us, event | category | flops | bytes accessed | tf_op | source)
XLA Modules:
  0.0 49.9 jit_solution(10424381306401519697)
XLA Ops:
  0.0 49.2 %shard_map.73 = f32[32,2,1024]{2,1,0:T(2,128)S(1)} custom-call(s32[2]{0:T(128)} %widths_far.1, f32[32,2,1024]{2,1,0:T(2,128)} %control.1, f32[32,4,2,1024]{3,2,1,0:T(2,128)} %ensemble.1, s32[4,4,2048]{2,1,0:T(4,128)} %source_far.1, f32[4,4,2048]{2,1,0:T(4,128)} %weight_far.1, s32[4,4,2048]{2,1,0:T(4,128)} %obs_mask_far.1, f32[4,4,2048]{2,1,0:T(4,128)} %innovation_far.1), custom_call_target="tpu_custom_call" | custom-call | tf_op jit(solution)/shard_map/pallas_call | solution.py:460
  49.2 0.7 %copy.9 = f32[32,2,1024]{2,1,0:T(2,128)} copy(f32[32,2,1024]{2,1,0:T(2,128)S(1)} %shard_map.73) | data formatting | bytes 524288

commit v5 on v4

--- a/solution.py
+++ b/solution.py
@@ -93,6 +93,23 @@
     has = (me_lat > 0, me_lat < lat_count - 1)
     beside = (me_lat - 1, me_lat + 1)
 
+    mates = [lax.rem(me_mem + d, mem_count) for d in range(mem_count)]
+    barrier = pltpu.get_barrier_semaphore()
+    for d in range(1, mem_count):
+        pl.semaphore_signal(barrier, inc=1, device_id={"mem": mates[d]}, device_id_type=MESH)
+    for side in range(2):
+
+        @pl.when(has[side])
+        def _():
+            for d in range(mem_count):
+                pl.semaphore_signal(
+                    barrier,
+                    inc=1,
+                    device_id={"mem": mates[d], "lat": beside[side]},
+                    device_id_type=MESH,
+                )
+
+    sides = has[0].astype(jnp.int32) + has[1].astype(jnp.int32)
     loads = []
 
     def load(src, dst):
@@ -113,25 +130,6 @@
         for r in range(rows):
             load(ensemble.at[:, t, r, :], ens.at[t, r])
 
-    mates = [lax.rem(me_mem + d, mem_count) for d in range(mem_count)]
-    barrier = pltpu.get_barrier_semaphore()
-    for d in range(1, mem_count):
-        pl.semaphore_signal(barrier, inc=1, device_id={"mem": mates[d]}, device_id_type=MESH)
-    for side in range(2):
-
-        @pl.when(has[side])
-        def _():
-            for d in range(mem_count):
-                pl.semaphore_signal(
-                    barrier,
-                    inc=1,
-                    device_id={"mem": mates[d], "lat": beside[side]},
-                    device_id_type=MESH,
-                )
-
-    sides = has[0].astype(jnp.int32) + has[1].astype(jnp.int32)
-    pl.semaphore_wait(barrier, mem_count - 1 + mem_count * sides)
-
     def send_to(where, src, dst, send, recv):
         return pltpu.make_async_remote_copy(
             src_ref=src,
@@ -210,6 +208,8 @@
         for r in range(rows):
             loads[1 + g * rows + r].wait()
             edge[0, r, part_of, :] = lon_filter(now[r, part_of, :], weights[r])
+        if g == 0:
+            pl.semaphore_wait(barrier, mem_count - 1 + mem_count * sides)
         edge_start(0, g)
 
     early = 1 + groups * rows + 4

time: 50.8 us -> 50.4 us (level)
  the two profiles are of different devices: /device:TPU:12 before, /device:TPU:9 now
where the time goes in v5:
time: 50.4 us; the launch traced here: 50.2 us
  Pallas kernels  49.5 us (98%)
  local copies, waits for them, and re-layouts  0.71 us (1%)
    pallas_call x1, Pallas kernels, local(): pl.pallas_call(functools.partial(kernel, (slots, members, rows, lon, mem_...  49.5 us

profile of v5, /device:TPU:9, one launch (start us, length us, event | category | flops | bytes accessed | tf_op | source)
XLA Modules:
  0.0 50.2 jit_solution(5094452255273485404)
XLA Ops:
  0.0 49.5 %shard_map.73 = f32[32,2,1024]{2,1,0:T(2,128)S(1)} custom-call(s32[2]{0:T(128)} %widths_far.1, f32[32,2,1024]{2,1,0:T(2,128)} %control.1, f32[32,4,2,1024]{3,2,1,0:T(2,128)} %ensemble.1, s32[4,4,2048]{2,1,0:T(4,128)} %source_far.1, f32[4,4,2048]{2,1,0:T(4,128)} %weight_far.1, s32[4,4,2048]{2,1,0:T(4,128)} %obs_mask_far.1, f32[4,4,2048]{2,1,0:T(4,128)} %innovation_far.1), custom_call_target="tpu_custom_call" | custom-call | tf_op jit(solution)/shard_map/pallas_call | solution.py:460
  49.5 0.7 %copy.9 = f32[32,2,1024]{2,1,0:T(2,128)} copy(f32[32,2,1024]{2,1,0:T(2,128)S(1)} %shard_map.73) | data formatting | bytes 524288
